TPU v7x, 256 devices: a whole 4x4x8 slice. The times are simulated.
256 devices in a mesh: gx: 32 (over x, z), gy: 8 (over y, core).
Axes of the slice: x: 4, y: 4, z: 8, core: 2. Of those that a mesh axis runs over, the one named last changes fastest.
Arguments:
- depth: float32 [4096, 4096], P('gx', 'gy'), may hold values from 0.3 to 1.2
- momentum_x: float32 [4096, 4096], P('gx', 'gy'), may hold values from -3 to 3
- momentum_y: float32 [4096, 4096], P('gx', 'gy'), may hold values from -3 to 3
- bed: float32 [4096, 4096], P('gx', 'gy'), may hold values from -1 to 1
- wet: int32 [4096, 4096], P('gx', 'gy'), may hold values 0 or 1
Outputs:
- new_depth: float32 [4096, 4096], P('gx', 'gy')
- velocity_x: float32 [4096, 4096], P('gx', 'gy')
- velocity_y: float32 [4096, 4096], P('gx', 'gy')
All inputs are finite; a program needn't handle non-finite values. No bound on the sum of `wet` on one device may be relied on, other than what follows from the above.
Results may differ from a plain program's by a relative error of at most 0.0013.
Values sent between devices are 32-bit elements; how exact they have to be, the bound alone decides.
A program may use at most 64 MiB of HBM per device.

v0:
```python
import jax
import jax.numpy as jnp
from jax import lax
from jax.sharding import PartitionSpec as P

gravity = 9.81
ratio_x = 0.05
ratio_y = 0.05


def with_halo(block, sides, width):
    for axis, dim in sides:
        count = lax.axis_size(axis)
        forward = [(i, i + 1) for i in range(count - 1)]
        backward = [(target, source) for source, target in forward]
        low = lax.ppermute(
            lax.slice_in_dim(block, block.shape[dim] - width, None, axis=dim), axis, forward
        )
        high = lax.ppermute(lax.slice_in_dim(block, 0, width, axis=dim), axis, backward)
        block = jnp.concatenate([low, block, high], axis=dim)
    return block


def minmod(left, right):
    return 0.5 * (jnp.sign(left) + jnp.sign(right)) * jnp.minimum(jnp.abs(left), jnp.abs(right))


def window(values, start, stop, line_axis):
    return lax.slice_in_dim(values, start, stop, axis=line_axis)


def physical(height, normal, across):
    speed_n = normal / height
    fluxes = (normal, normal * speed_n + 0.5 * gravity * height * height, across * speed_n)
    return (fluxes, jnp.abs(speed_n) + jnp.sqrt(gravity * height))


def face_terms(depth, normal, across, wet_cells, line_axis):
    length = depth.shape[line_axis]
    states = (depth, normal, across)
    slopes = [
        minmod(
            window(field, 1, length - 1, line_axis) - window(field, 0, length - 2, line_axis),
            window(field, 2, length, line_axis) - window(field, 1, length - 1, line_axis),
        )
        for field in states
    ]
    lefts = [
        window(field, 1, length - 2, line_axis) + 0.5 * window(slope, 0, length - 3, line_axis)
        for field, slope in zip(states, slopes)
    ]
    rights = [
        window(field, 2, length - 1, line_axis) - 0.5 * window(slope, 1, length - 2, line_axis)
        for field, slope in zip(states, slopes)
    ]
    opened = window(wet_cells, 1, length - 2, line_axis) * window(
        wet_cells, 2, length - 1, line_axis
    )
    safe_left = jnp.where(opened > 0.5, lefts[0], 1.0)
    safe_right = jnp.where(opened > 0.5, rights[0], 1.0)
    flux_left, speed_left = physical(safe_left, lefts[1], lefts[2])
    flux_right, speed_right = physical(safe_right, rights[1], rights[2])
    fastest = jnp.maximum(speed_left, speed_right)
    result = []
    for flux_a, flux_b, state_a, state_b in zip(flux_left, flux_right, lefts, rights):
        face = opened * (0.5 * (flux_a + flux_b) - 0.5 * fastest * (state_b - state_a))
        count = face.shape[line_axis]
        result.append(window(face, 1, count, line_axis) - window(face, 0, count - 1, line_axis))
    return result


def predict(padded):
    along_x = padded[:, :, 2:-2]
    along_y = padded[:, 2:-2, :]
    center = padded[:, 2:-2, 2:-2]
    depth, flow_x, flow_y, wet_cells = (center[0], center[1], center[2], center[4])
    mass_x, normal_x, shear_x = face_terms(along_x[0], along_x[1], along_x[2], along_x[4], 0)
    mass_y, normal_y, shear_y = face_terms(along_y[0], along_y[2], along_y[1], along_y[4], 1)
    bed_x = 0.5 * (along_x[3, 3:-1] - along_x[3, 1:-3])
    bed_y = 0.5 * (along_y[3, :, 3:-1] - along_y[3, :, 1:-3])
    new_depth = depth - wet_cells * (ratio_x * mass_x + ratio_y * mass_y)
    push_x = wet_cells * (
        flow_x - ratio_x * normal_x - ratio_y * shear_y - ratio_x * gravity * depth * bed_x
    )
    push_y = wet_cells * (
        flow_y - ratio_x * shear_x - ratio_y * normal_y - ratio_y * gravity * depth * bed_y
    )
    return (new_depth, push_x, push_y)


def earlier(values, stride, line_axis, fill):
    which = line_axis % values.ndim
    widths = [(0, 0)] * values.ndim
    widths[which] = (stride, 0)
    padded = jnp.pad(values, widths, constant_values=fill)
    return lax.slice_in_dim(padded, 0, values.shape[which], axis=which)


def later(values, stride, line_axis, fill):
    which = line_axis % values.ndim
    widths = [(0, 0)] * values.ndim
    widths[which] = (0, stride)
    padded = jnp.pad(values, widths, constant_values=fill)
    return lax.slice_in_dim(padded, stride, stride + values.shape[which], axis=which)


def eliminate(rows, below, above):
    lower, diagonal, upper, right = rows
    left_factor = lower / below[1]
    right_factor = upper / above[1]
    return (
        -left_factor * below[0],
        diagonal - left_factor * below[2] - right_factor * above[0],
        -right_factor * above[2],
        right - left_factor * below[3] - right_factor * above[3],
    )


def reduce_lines(lower, diagonal, upper, right, line_axis):
    count = diagonal.shape[line_axis % diagonal.ndim]
    rows = (lower, diagonal, upper, right)
    stride = 1
    while stride < count:
        below = tuple(
            (
                earlier(member, stride, line_axis, fill)
                for member, fill in zip(rows, (0.0, 1.0, 0.0, 0.0))
            )
        )
        above = tuple(
            (
                later(member, stride, line_axis, fill)
                for member, fill in zip(rows, (0.0, 1.0, 0.0, 0.0))
            )
        )
        rows = lax.optimization_barrier(eliminate(rows, below, above))
        stride *= 2
    return rows[3] / rows[1]


def separator_rows(last_six, next_three):
    solved_y, solved_g, solved_e, sep_coef, sep_diag, sep_right = last_six
    first_y, first_g, first_e = next_three
    return (
        -sep_coef * solved_g,
        sep_diag - sep_coef * solved_e - sep_coef * first_g,
        -sep_coef * first_e,
        sep_right + sep_coef * solved_y + sep_coef * first_y,
    )


def local_spikes(coefficient, right, line_axis):
    which = line_axis % 2
    count = coefficient.shape[which]
    inner = lax.slice_in_dim(coefficient, 0, count - 1, axis=which)
    position = lax.broadcasted_iota(jnp.int32, inner.shape, which)
    zeros = jnp.zeros_like(inner)
    sources = jnp.stack(
        [
            lax.slice_in_dim(right, 0, count - 1, axis=which),
            jnp.where(position == 0, inner, zeros),
            jnp.where(position == count - 2, inner, zeros),
        ]
    )
    solved = reduce_lines(-inner, 1.0 + 2.0 * inner, -inner, sources, line_axis)
    first = lax.index_in_dim(solved, 0, which + 1, keepdims=False)
    final = lax.index_in_dim(solved, count - 2, which + 1, keepdims=False)
    sep_coef = lax.index_in_dim(coefficient, count - 1, which, keepdims=False)
    sep_right = lax.index_in_dim(right, count - 1, which, keepdims=False)
    last_six = jnp.concatenate([final, jnp.stack([sep_coef, 1.0 + 2.0 * sep_coef, sep_right])])
    return (solved, first, last_six)


def assemble(solved, own, previous, line_axis):
    which = line_axis % 2
    own_wide = jnp.expand_dims(own, which)
    prev_wide = jnp.expand_dims(previous, which)
    inner = solved[0] + solved[1] * prev_wide + solved[2] * own_wide
    return jnp.concatenate([inner, own_wide], axis=which)


def pick_rows(whole, index):
    first_all = whole[:3]
    rows = separator_rows(whole[3:], later(first_all, 1, -2, 0.0))
    solved = reduce_lines(rows[0], rows[1], rows[2], rows[3], -2)
    own = lax.dynamic_index_in_dim(solved, index, 0, keepdims=False)
    previous = lax.dynamic_index_in_dim(earlier(solved, 1, -2, 0.0), index, 0, keepdims=False)
    return (own, previous)


def interface_x(first, last_six):
    packed = jnp.concatenate([first, last_six])[:, None, :]
    whole = lax.all_gather(packed, "gx", axis=1, tiled=True)
    return pick_rows(whole, lax.axis_index("gx"))


def interface_y(first, last_six):
    packed = jnp.concatenate([first, last_six])[:, None, :]
    whole = lax.all_gather(packed, "gy", axis=1, tiled=True)
    return pick_rows(whole, lax.axis_index("gy"))


def on_device(depth, momentum_x, momentum_y, bed, wet):
    stacked = jnp.stack([depth, momentum_x, momentum_y, bed, wet.astype(jnp.float32)])
    padded = with_halo(stacked, (("gx", 1), ("gy", 2)), 2)
    new_depth, push_x, push_y = predict(padded)
    cells_x = depth.shape[0] * lax.axis_size("gx")
    cells_y = depth.shape[1] * lax.axis_size("gy")
    scale_x = (cells_x / 4.0) ** 2 / 3.0
    scale_y = (cells_y / 4.0) ** 2 / 3.0
    coef_x = scale_x * depth * depth
    coef_y = scale_y * depth * depth
    solved_x, first_x, last_x = local_spikes(coef_x, push_x, -2)
    own_x, prev_x = interface_x(first_x, last_x)
    flux_u = assemble(solved_x, own_x, prev_x, -2)
    solved_y, first_y, last_y = local_spikes(coef_y, push_y, -1)
    own_y, prev_y = interface_y(first_y, last_y)
    flux_v = assemble(solved_y, own_y, prev_y, -1)
    return (new_depth, flux_u / depth, flux_v / depth)


def solution(mesh):
    placed = (P("gx", "gy"), P("gx", "gy"), P("gx", "gy"), P("gx", "gy"), P("gx", "gy"))
    return jax.shard_map(
        on_device,
        mesh=mesh,
        in_specs=placed,
        out_specs=(P("gx", "gy"), P("gx", "gy"), P("gx", "gy")),
        check_vma=False,
    )
```

profile of v0, /device:TPU:8, one launch (start us, length us, event | category | flops | bytes accessed | tf_op | source)
XLA Modules:
  0.0 121.2 jit_solution(9153613067700028402)
XLA Ops:
  0.7 1.0 bitcast_dynamic-update-slice_fusion.4
  1.7 1.0 bitcast_dynamic-update-slice_fusion.3
  2.7 1.0 bitcast_dynamic-update-slice_fusion.2
  3.7 3.8 %collective-permute-start = (f32[5,2,512]{2,1,0:T(2,128)S(1)}, f32[5,2,512]{2,1,0:T(2,128)S(1)}, u32[]{:S(2)}, u32[]{:S(2)}) collective-permute-start(f32[5,2,512]{2,1,0:T(2,128)S(1)} %get-tuple-element.274), channel_id=1, source_target_pairs={{0,8},{8,16},{16,24},{24,32},{32,40},{40,48},{48,56},{56,64},{64,7... | collective-permute-start | bytes 61448 | tf_op jit(solution)/shard_map/ppermute | solution.py:16
  7.6 1.3 %collective-permute-start.1 = (f32[5,2,512]{2,1,0:T(2,128)S(1)}, f32[5,2,512]{2,1,0:T(2,128)S(1)}, u32[]{:S(2)}, u32[]{:S(2)}) collective-permute-start(f32[5,2,512]{2,1,0:T(2,128)S(1)} %get-tuple-element.275), channel_id=1, source_target_pairs={{8,0},{16,8},{24,16},{32,24},{40,32},{48,40},{56,48},{64,56},{72,6... | collective-permute-start | bytes 61448 | tf_op jit(solution)/shard_map/ppermute | solution.py:19
  9.5 3.8 %collective-permute-done.1 = f32[5,2,512]{2,1,0:T(2,128)S(1)} collective-permute-done((f32[5,2,512]{2,1,0:T(2,128)S(1)}, f32[5,2,512]{2,1,0:T(2,128)S(1)}, u32[]{:S(2)}, u32[]{:S(2)}) %collective-permute-start.1) | collective-permute-done | bytes 20512 | tf_op jit(solution)/shard_map/ppermute | solution.py:19
  13.7 1.9 %collective-permute-start.2 = (f32[5,132,2]{2,1,0:T(8,128)S(1)}, f32[5,132,2]{2,1,0:T(8,128)S(1)}, u32[]{:S(2)}, u32[]{:S(2)}) collective-permute-start(f32[5,132,2]{2,1,0:T(8,128)S(1)} %get-tuple-element.272), channel_id=1, source_target_pairs={{0,1},{1,2},{2,3},{3,4},{4,5},{5,6},{6,7},{8,9},{9,10},{10,11},{11... | collective-permute-start | bytes 15848 | tf_op jit(solution)/shard_map/ppermute | solution.py:16
  15.6 3.6 %collective-permute-start.3 = (f32[5,132,2]{2,1,0:T(8,128)S(1)}, f32[5,132,2]{2,1,0:T(8,128)S(1)}, u32[]{:S(2)}, u32[]{:S(2)}) collective-permute-start(f32[5,132,2]{2,1,0:T(8,128)S(1)} %get-tuple-element.273), channel_id=1, source_target_pairs={{1,0},{2,1},{3,2},{4,3},{5,4},{6,5},{7,6},{9,8},{10,9},{11,10},{12... | collective-permute-start | bytes 15848 | tf_op jit(solution)/shard_map/ppermute | solution.py:19
  19.3 1.5 %minimum_multiply_fusion.4 = (f32[1,130,512]{2,1,0:T(8,128)S(1)}, f32[1,130,512]{2,1,0:T(8,128)S(1)}, f32[1,130,512]{2,1,0:T(8,128)S(1)}) fusion(f32[5,2,512]{2,1,0:T(2,128)} %copy-done.15, f32[5,128,512]{2,1,0:T(8,128)S(1)} %bitcast_dynamic-update-slice_fusion, f32[5,2,512]{2,1,0:T(2,128)} %copy-done.12, f32[5,132,512]{2,1,0:T(8,128)S(1)} %pad_maximum_fusion), kind=kLoop, calls=%fused_computation.293 | loop fusion | flops 2396160 | bytes 2949120 | tf_op jit(solution)/shard_map/mul | solution.py:25
  21.4 1.2 fusion.73
  22.5 1.5 %collective-permute-done.3 = f32[5,132,2]{2,1,0:T(8,128)S(1)} collective-permute-done((f32[5,132,2]{2,1,0:T(8,128)S(1)}, f32[5,132,2]{2,1,0:T(8,128)S(1)}, u32[]{:S(2)}, u32[]{:S(2)}) %collective-permute-start.3) | collective-permute-done | bytes 5312 | tf_op jit(solution)/shard_map/ppermute | solution.py:19
  24.8 1.3 %minimum_multiply_fusion = (f32[128,514]{1,0:T(8,128)}, f32[128,514]{1,0:T(8,128)S(1)}) fusion(f32[128,516]{1,0:T(8,128)S(1)} %get-tuple-element.267, f32[128,516]{1,0:T(8,128)S(1)} %get-tuple-element.268), kind=kLoop, calls=%fused_computation.214 | loop fusion | flops 1315840 | bytes 2105344 | tf_op jit(solution)/shard_map/mul | solution.py:25
  26.2 0.8 subtract_multiply_fusion.1
  27.0 0.8 fusion.60
  28.1 1.1 fusion.232
  39.0 0.9 copy-done
  40.7 1.3 %concatenate.52 = f32[9,128]{1,0:T(8,128)S(1)} concatenate(f32[3,128]{1,0:T(4,128)S(1)} %get-tuple-element.189, f32[3,128]{1,0:T(4,128)S(1)} %get-tuple-element.188, f32[1,128]{1,0:T(1,128)} %bitcast.173, f32[1,128]{1,0:T(1,128)} %multiply_add_fusion.3, f32[1,128]{1,0:T(1,128)} %bitcast.174), dimensions={0} | concatenate | bytes 9216 | tf_op jit(solution)/shard_map/concatenate | solution.py:198
  42.0 13.1 %all-gather.1 = f32[9,1024]{1,0:T(8,128)S(1)} all-gather(f32[9,128]{1,0:T(8,128)S(1)} %concatenate.52), channel_id=3, replica_groups=mesh['gx'=32,'gy'=8] {'gy'}, dimensions={1}, use_global_device_ids=true | all-gather | bytes 41472 | tf_op jit(solution)/shard_map/all_gather | solution.py:199
  55.1 0.9 multiply_add_fusion.1
  56.0 1.8 %subtract_multiply_fusion = f32[128,513]{1,0:T(8,128)} fusion(f32[128,514]{1,0:T(8,128)S(1)} %copy-done.4, f32[128,516]{1,0:T(8,128)S(1)} %get-tuple-element.267, f32[128,516]{1,0:T(8,128)S(1)} %maximum_bitcast_fusion.2, f32[128,514]{1,0:T(8,128)S(1)} %minimum_multiply_fusion.2, f32[128,516]{1,0:T(8,128)S(1)} %get-tuple-element.269, ...), kind=kLoop, calls=%fused_computation.213 | loop fusion | flops 2232576 | bytes 3939840 | tf_op jit(solution)/shard_map/mul | solution.py:66
  58.7 1.2 fusion.224
  60.0 2.0 %maximum_divide_fusion.1 = (f32[128,512]{1,0:T(8,128)}, f32[128,512]{1,0:T(8,128)S(1)}) fusion(f32[128,512]{1,0:T(8,128)S(1)} %copy-done.3, f32[128,1]{1,0:T(8,128)} %copy.28, f32[128,511]{1,0:T(8,128)S(1)} %fusion.224, f32[5,128,512]{2,1,0:T(8,128)S(1)} %bitcast_dynamic-update-slice_fusion, f32[5,2,512]{2,1,0:T(2,128)S(1)} %copy-done.14, ...), kind=kLoop, calls=%fused_computation.461 | loop fusion | flops 1114112 | bytes 3973120 | tf_op jit(solution)/shard_map/div | solution.py:219
  65.2 53.4 %all-gather = f32[9,16384]{1,0:T(8,128)S(1)} all-gather(f32[9,512]{1,0:T(8,128)S(1)} %concatenate.48), channel_id=2, replica_groups=mesh['gx'=32,'gy'=8] {'gx'}, dimensions={1}, use_global_device_ids=true | all-gather | bytes 608256 | tf_op jit(solution)/shard_map/all_gather | solution.py:193
  118.6 1.0 slice_reduce_fusion.4
  (167 shorter events, 18.5 us)
Async XLA Ops:
  0.6 3.0 %copy-start.18 = (f32[128,512]{1,0:T(8,128)S(1)}, f32[128,512]{1,0:T(8,128)}, u32[]{:S(2)}) copy-start(f32[128,512]{1,0:T(8,128)} %param.8) | copy-start | bytes 786436
  0.6 3.0 %copy-start.6 = (s32[128,512]{1,0:T(8,128)S(1)}, s32[128,512]{1,0:T(8,128)}, u32[]{:S(2)}) copy-start(s32[128,512]{1,0:T(8,128)} %param.9) | copy-start | bytes 786436
  3.7 5.7 %collective-permute-start = (f32[5,2,512]{2,1,0:T(2,128)S(1)}, f32[5,2,512]{2,1,0:T(2,128)S(1)}, u32[]{:S(2)}, u32[]{:S(2)}) collective-permute-start(f32[5,2,512]{2,1,0:T(2,128)S(1)} %get-tuple-element.274), channel_id=1, source_target_pairs={{0,8},{8,16},{16,24},{24,32},{32,40},{40,48},{48,56},{56,64},{64,7... | collective-permute-start | bytes 61448 | tf_op jit(solution)/shard_map/ppermute | solution.py:16
  7.6 5.7 %collective-permute-start.1 = (f32[5,2,512]{2,1,0:T(2,128)S(1)}, f32[5,2,512]{2,1,0:T(2,128)S(1)}, u32[]{:S(2)}, u32[]{:S(2)}) collective-permute-start(f32[5,2,512]{2,1,0:T(2,128)S(1)} %get-tuple-element.275), channel_id=1, source_target_pairs={{8,0},{16,8},{24,16},{32,24},{40,32},{48,40},{56,48},{64,56},{72,6... | collective-permute-start | bytes 61448 | tf_op jit(solution)/shard_map/ppermute | solution.py:19
  9.5 6.1 %copy-start.12 = (f32[5,2,512]{2,1,0:T(2,128)}, f32[5,2,512]{2,1,0:T(2,128)S(1)}, u32[]{:S(2)}) copy-start(f32[5,2,512]{2,1,0:T(2,128)S(1)} %collective-permute-done) | copy-start | bytes 61444
  13.2 2.4 %copy-start.15 = (f32[5,2,512]{2,1,0:T(2,128)}, f32[5,2,512]{2,1,0:T(2,128)S(1)}, u32[]{:S(2)}) copy-start(f32[5,2,512]{2,1,0:T(2,128)S(1)} %collective-permute-done.1) | copy-start | bytes 61444
  13.7 8.9 %collective-permute-start.2 = (f32[5,132,2]{2,1,0:T(8,128)S(1)}, f32[5,132,2]{2,1,0:T(8,128)S(1)}, u32[]{:S(2)}, u32[]{:S(2)}) collective-permute-start(f32[5,132,2]{2,1,0:T(8,128)S(1)} %get-tuple-element.272), channel_id=1, source_target_pairs={{0,1},{1,2},{2,3},{3,4},{4,5},{5,6},{6,7},{8,9},{9,10},{10,11},{11... | collective-permute-start | bytes 15848 | tf_op jit(solution)/shard_map/ppermute | solution.py:16
  15.6 8.4 %collective-permute-start.3 = (f32[5,132,2]{2,1,0:T(8,128)S(1)}, f32[5,132,2]{2,1,0:T(8,128)S(1)}, u32[]{:S(2)}, u32[]{:S(2)}) collective-permute-start(f32[5,132,2]{2,1,0:T(8,128)S(1)} %get-tuple-element.273), channel_id=1, source_target_pairs={{1,0},{2,1},{3,2},{4,3},{5,4},{6,5},{7,6},{9,8},{10,9},{11,10},{12... | collective-permute-start | bytes 15848 | tf_op jit(solution)/shard_map/ppermute | solution.py:19
  19.3 1.5 %copy-start.13 = (f32[5,2,512]{2,1,0:T(2,128)S(1)}, f32[5,2,512]{2,1,0:T(2,128)}, u32[]{:S(2)}) copy-start(f32[5,2,512]{2,1,0:T(2,128)} %copy-done.12) | copy-start | bytes 61444
  19.3 1.5 %copy-start.16 = (f32[5,2,512]{2,1,0:T(2,128)S(1)}, f32[5,2,512]{2,1,0:T(2,128)}, u32[]{:S(2)}) copy-start(f32[5,2,512]{2,1,0:T(2,128)} %copy-done.15) | copy-start | bytes 61444
  27.0 1.0 copy-start.7
  27.0 1.1 copy-start.11
  29.4 10.8 %copy-start.19 = (f32[128]{0:T(128)}, f32[128]{0:T(128)S(1)}, u32[]{:S(2)}) copy-start(f32[128]{0:T(128)S(1)} %slice_reduce_fusion.3) | copy-start | bytes 1540
  42.0 14.0 %copy-start.4 = (f32[128,514]{1,0:T(8,128)S(1)}, f32[128,514]{1,0:T(8,128)}, u32[]{:S(2)}) copy-start(f32[128,514]{1,0:T(8,128)} %get-tuple-element.331) | copy-start | bytes 789508
  57.8 2.1 %copy-start.3 = (f32[128,512]{1,0:T(8,128)S(1)}, f32[128,512]{1,0:T(8,128)}, u32[]{:S(2)}) copy-start(f32[128,512]{1,0:T(8,128)} %param.5) | copy-start | bytes 786436
  57.8 2.2 %copy-start.8 = (s32[128,512]{1,0:T(8,128)S(1)}, s32[128,512]{1,0:T(8,128)}, u32[]{:S(2)}) copy-start(s32[128,512]{1,0:T(8,128)} %param.9) | copy-start | bytes 786436
  57.8 2.2 %copy-start.9 = (f32[129,512]{1,0:T(8,128)S(1)}, f32[129,512]{1,0:T(8,128)}, u32[]{:S(2)}) copy-start(f32[129,512]{1,0:T(8,128)} %get-tuple-element.270) | copy-start | bytes 792580
  57.8 2.2 %copy-start.10 = (f32[128,513]{1,0:T(8,128)S(1)}, f32[128,513]{1,0:T(8,128)}, u32[]{:S(2)}) copy-start(f32[128,513]{1,0:T(8,128)} %subtract_multiply_fusion) | copy-start | bytes 787972
  57.8 2.2 %copy-start.14 = (f32[5,2,512]{2,1,0:T(2,128)S(1)}, f32[5,2,512]{2,1,0:T(2,128)}, u32[]{:S(2)}) copy-start(f32[5,2,512]{2,1,0:T(2,128)} %copy-done.12) | copy-start | bytes 61444
  57.8 2.2 %copy-start.17 = (f32[5,2,512]{2,1,0:T(2,128)S(1)}, f32[5,2,512]{2,1,0:T(2,128)}, u32[]{:S(2)}) copy-start(f32[5,2,512]{2,1,0:T(2,128)} %copy-done.15) | copy-start | bytes 61444
  60.0 2.1 %copy-start.1 = (f32[127,512]{1,0:T(8,128)S(1)}, f32[127,512]{1,0:T(8,128)}, u32[]{:S(2)}) copy-start(f32[127,512]{1,0:T(8,128)} %get-tuple-element.294) | copy-start | bytes 780292
  60.0 2.1 %copy-start.5 = (f32[127,512]{1,0:T(8,128)S(1)}, f32[127,512]{1,0:T(8,128)}, u32[]{:S(2)}) copy-start(f32[127,512]{1,0:T(8,128)} %get-tuple-element.293) | copy-start | bytes 780292
  60.0 2.1 %copy-start.20 = (pred[127]{0:T(512)(128)(4,1)S(1)}, pred[127]{0:T(512)(128)(4,1)}, u32[]{:S(2)}) copy-start(pred[127]{0:T(512)(128)(4,1)} %get-tuple-element.333) | copy-start | bytes 385
  60.0 2.1 %copy-start.21 = (pred[127]{0:T(512)(128)(4,1)S(1)}, pred[127]{0:T(512)(128)(4,1)}, u32[]{:S(2)}) copy-start(pred[127]{0:T(512)(128)(4,1)} %get-tuple-element.334) | copy-start | bytes 385
  (2 other events, 1.9 us)
where the time goes:
time: 122 us; the launch traced here: 121 us
  blocking collectives  66.5 us (55%)
  other arithmetic  28 us (23%)
  starting transfers between devices  10.7 us (9%)
  local copies, waits for them, and re-layouts  9.07 us (7%)
  waiting for transfers between devices  5.26 us (4%)
  between operations  1.77 us (1%)
    all_gather x1, blocking collectives, interface_x(): whole = lax.all_gather(packed, 'gx', axis=1, tiled=True)  53.4 us
    all_gather x1, blocking collectives, interface_y(): whole = lax.all_gather(packed, 'gy', axis=1, tiled=True)  13.1 us
    ppermute x2, starting transfers between devices, with_halo(): lax.ppermute(lax.slice_in_dim(block, block.shape[dim] - width, None, axis...  5.74 us
    ppermute x2, waiting for transfers between devices, with_halo(): lax.ppermute(lax.slice_in_dim(block, 0, width, axis=dim), axis, backward)  5.26 us
    sub x24, other arithmetic, eliminate(): right - left_factor * below[3] - right_factor * above[3]  5.16 us
    mul x5, other arithmetic, face_terms(): opened * (0.5 * (flux_a + flux_b) - 0.5 * fastest * (state_b - state_a))  5.04 us
    ppermute x2, starting transfers between devices, with_halo(): lax.ppermute(lax.slice_in_dim(block, 0, width, axis=dim), axis, backward)  4.93 us
    unnamed x53, local copies, waits for them, and re-layouts  4.38 us
  transfers between devices with their start and end apart: 4, of which 2 were waited for; matrix products, arithmetic and copies ran while one was open for 3% of the time, Pallas kernels for 0%

commit v1 on v0

--- a/solution.py
+++ b/solution.py
@@ -196,7 +196,9 @@
 
 def interface_y(first, last_six):
     packed = jnp.concatenate([first, last_six])[:, None, :]
-    whole = lax.all_gather(packed, "gy", axis=1, tiled=True)
+    whole = jnp.concatenate(
+        lax.all_to_all(jnp.stack([packed] * lax.axis_size("gy")), "gy", 0, 0), axis=1
+    )
     return pick_rows(whole, lax.axis_index("gy"))
 
 

time: 122 us -> 115 us (0.943)
  blocking collectives: 66.5 us -> 53.4 us
  starting transfers between devices: 10.7 us -> 16.8 us
  waiting for transfers between devices: 5.26 us -> 8.22 us
  other arithmetic: 28 us -> 25.4 us
    all_gather x1 -> x0, blocking collectives: 13.1 us -> none  [interface_y(): whole = lax.all_gather(packed, 'gy', axis=1, tiled=True)]
    all_to_all x0 -> x1, starting transfers between devices: none -> 6.08 us  [interface_y(): lax.all_to_all(jnp.stack([packed] * lax.axis_size('gy')), 'gy', 0, 0)]
    all_to_all x0 -> x1, waiting for transfers between devices: none -> 1.56 us  [interface_y(): lax.all_to_all(jnp.stack([packed] * lax.axis_size('gy')), 'gy', 0, 0)]
    mul x3, other arithmetic: 3.05 us -> 1.59 us  [minmod(): 0.5 * (jnp.sign(left) + jnp.sign(right))]
    concatenate x1, local copies, waits for them, and re-layouts: 1.31 us -> 0.04 us  [interface_y(): packed = jnp.concatenate([first, last_six])[:, None, :]]
    unnamed x53 -> x30, local copies, waits for them, and re-layouts: 4.38 us -> 5.64 us
  transfers between devices with their start and end apart: 4 -> 5, of which waited for: 2 -> 5; matrix products, arithmetic and copies ran while one was open for 3% -> 4% of each run, Pallas kernels for 0% -> 0%
where the time goes in v1:
time: 115 us; the launch traced here: 114 us
  blocking collectives  53.4 us (46%)
  other arithmetic  25.4 us (22%)
  starting transfers between devices  16.8 us (15%)
  local copies, waits for them, and re-layouts  8.53 us (7%)
  waiting for transfers between devices  8.22 us (7%)
  between operations  1.62 us (1%)
    all_gather x1, blocking collectives, interface_x(): whole = lax.all_gather(packed, 'gx', axis=1, tiled=True)  53.4 us
    all_to_all x1, starting transfers between devices, interface_y(): lax.all_to_all(jnp.stack([packed] * lax.axis_size('gy')), 'gy', 0, 0)  6.08 us
    ppermute x2, waiting for transfers between devices, with_halo(): lax.ppermute(lax.slice_in_dim(block, 0, width, axis=dim), axis, backward)  5.97 us
    ppermute x2, starting transfers between devices, with_halo(): lax.ppermute(lax.slice_in_dim(block, block.shape[dim] - width, None, axis...  5.74 us
    unnamed x30, local copies, waits for them, and re-layouts  5.64 us
    sub x24, other arithmetic, eliminate(): right - left_factor * below[3] - right_factor * above[3]  5.22 us
    mul x5, other arithmetic, face_terms(): opened * (0.5 * (flux_a + flux_b) - 0.5 * fastest * (state_b - state_a))  4.99 us
    ppermute x2, starting transfers between devices, with_halo(): lax.ppermute(lax.slice_in_dim(block, 0, width, axis=dim), axis, backward)  4.93 us
  transfers between devices with their start and end apart: 5, of which 5 were waited for; matrix products, arithmetic and copies ran while one was open for 4% of the time, Pallas kernels for 0%

profile of v1, /device:TPU:8, one launch (start us, length us, event | category | flops | bytes accessed | tf_op | source)
XLA Modules:
  0.0 113.9 jit_solution(15939293743457586420)
XLA Ops:
  0.7 1.0 bitcast_dynamic-update-slice_fusion.4
  1.7 1.0 bitcast_dynamic-update-slice_fusion.3
  2.7 1.0 bitcast_dynamic-update-slice_fusion.2
  3.7 3.8 %collective-permute-start = (f32[5,2,512]{2,1,0:T(2,128)S(1)}, f32[5,2,512]{2,1,0:T(2,128)S(1)}, u32[]{:S(2)}, u32[]{:S(2)}) collective-permute-start(f32[5,2,512]{2,1,0:T(2,128)S(1)} %get-tuple-element.274), channel_id=1, source_target_pairs={{0,8},{8,16},{16,24},{24,32},{32,40},{40,48},{48,56},{56,64},{64,7... | collective-permute-start | bytes 61448 | tf_op jit(solution)/shard_map/ppermute | solution.py:16
  7.6 1.3 %collective-permute-start.1 = (f32[5,2,512]{2,1,0:T(2,128)S(1)}, f32[5,2,512]{2,1,0:T(2,128)S(1)}, u32[]{:S(2)}, u32[]{:S(2)}) collective-permute-start(f32[5,2,512]{2,1,0:T(2,128)S(1)} %get-tuple-element.275), channel_id=1, source_target_pairs={{8,0},{16,8},{24,16},{32,24},{40,32},{48,40},{56,48},{64,56},{72,6... | collective-permute-start | bytes 61448 | tf_op jit(solution)/shard_map/ppermute | solution.py:19
  9.0 4.2 %collective-permute-done.1 = f32[5,2,512]{2,1,0:T(2,128)S(1)} collective-permute-done((f32[5,2,512]{2,1,0:T(2,128)S(1)}, f32[5,2,512]{2,1,0:T(2,128)S(1)}, u32[]{:S(2)}, u32[]{:S(2)}) %collective-permute-start.1) | collective-permute-done | bytes 20512 | tf_op jit(solution)/shard_map/ppermute | solution.py:19
  13.6 1.9 %collective-permute-start.2 = (f32[5,132,2]{2,1,0:T(8,128)S(1)}, f32[5,132,2]{2,1,0:T(8,128)S(1)}, u32[]{:S(2)}, u32[]{:S(2)}) collective-permute-start(f32[5,132,2]{2,1,0:T(8,128)S(1)} %get-tuple-element.272), channel_id=1, source_target_pairs={{0,1},{1,2},{2,3},{3,4},{4,5},{5,6},{6,7},{8,9},{9,10},{10,11},{11... | collective-permute-start | bytes 15848 | tf_op jit(solution)/shard_map/ppermute | solution.py:16
  15.5 3.6 %collective-permute-start.3 = (f32[5,132,2]{2,1,0:T(8,128)S(1)}, f32[5,132,2]{2,1,0:T(8,128)S(1)}, u32[]{:S(2)}, u32[]{:S(2)}) collective-permute-start(f32[5,132,2]{2,1,0:T(8,128)S(1)} %get-tuple-element.273), channel_id=1, source_target_pairs={{1,0},{2,1},{3,2},{4,3},{5,4},{6,5},{7,6},{9,8},{10,9},{11,10},{12... | collective-permute-start | bytes 15848 | tf_op jit(solution)/shard_map/ppermute | solution.py:19
  20.5 1.1 %fusion.73 = (f32[129,512]{1,0:T(8,128)}, f32[129,512]{1,0:T(8,128)S(1)}) fusion(f32[129,512]{1,0:T(8,128)S(1)} %get-tuple-element.229, f32[129,512]{1,0:T(8,128)S(1)} %get-tuple-element.225, f32[129,512]{1,0:T(8,128)S(1)} %get-tuple-element.226, f32[129,512]{1,0:T(8,128)S(1)} %get-tuple-element.228, f32[129,512]{1,0:T(8,128)S(1)} %get-tuple-element.227), kind=kLoop, calls=%fused_computation.229 | loop fusion | flops 2179584 | bytes 1849344 | tf_op jit(solution)/shard_map/mul | solution.py:66
  22.2 1.8 %collective-permute-done.3 = f32[5,132,2]{2,1,0:T(8,128)S(1)} collective-permute-done((f32[5,132,2]{2,1,0:T(8,128)S(1)}, f32[5,132,2]{2,1,0:T(8,128)S(1)}, u32[]{:S(2)}, u32[]{:S(2)}) %collective-permute-start.3) | collective-permute-done | bytes 5312 | tf_op jit(solution)/shard_map/ppermute | solution.py:19
  25.4 0.8 subtract_multiply_fusion.1
  26.2 0.8 fusion.60
  27.2 1.1 fusion.232
  28.8 1.7 %subtract_multiply_fusion = f32[128,513]{1,0:T(8,128)} fusion(f32[128,514]{1,0:T(8,128)S(1)} %get-tuple-element.331, f32[128,516]{1,0:T(8,128)S(1)} %get-tuple-element.267, f32[128,516]{1,0:T(8,128)S(1)} %maximum_bitcast_fusion.2, f32[128,514]{1,0:T(8,128)S(1)} %minimum_multiply_fusion.2, f32[128,516]{1,0:T(8,128)S(1)} %get-tuple-element.269, ...), kind=kLoop, calls=%fused_computation.213 | loop fusion | flops 2232576 | bytes 3939840 | tf_op jit(solution)/shard_map/mul | solution.py:66
  40.4 6.1 %all-to-all-start = ((f32[8,9,1,128]{3,2,1,0:T(1,128)}), f32[8,9,1,128]{3,2,1,0:T(1,128)S(1)}, u32[]{:S(2)}, u32[]{:S(2)}) async-start(f32[8,9,1,128]{3,2,1,0:T(1,128)} %stack.61), calls=%async_computation | async-start | bytes 73728 | tf_op jit(solution)/shard_map/all_to_all | solution.py:200
  46.5 0.9 negate_multiply_fusion.2
  47.4 0.8 multiply_subtract_fusion.3
  49.0 1.6 %all-to-all-done = f32[8,9,1,128]{3,2,1,0:T(1,128)S(1)} async-done(((f32[8,9,1,128]{3,2,1,0:T(1,128)}), f32[8,9,1,128]{3,2,1,0:T(1,128)S(1)}, u32[]{:S(2)}, u32[]{:S(2)}) %all-to-all-start) | async-done | bytes 36896 | tf_op jit(solution)/shard_map/all_to_all | solution.py:200
  51.0 2.4 %maximum_divide_fusion.1 = (f32[128,512]{1,0:T(8,128)}, f32[128,512]{1,0:T(8,128)S(1)}) fusion(f32[128,512]{1,0:T(8,128)S(1)} %copy-done, f32[128,1]{1,0:T(8,128)S(1)} %copy.35, f32[128,511]{1,0:T(8,128)S(1)} %fusion.224, f32[5,128,512]{2,1,0:T(8,128)S(1)} %bitcast_dynamic-update-slice_fusion, f32[5,2,512]{2,1,0:T(2,128)S(1)} %collective-permute-done, ...), kind=kLoop, calls=%fused_computation.461 | loop fusion | flops 1114112 | bytes 3973120 | tf_op jit(solution)/shard_map/div | solution.py:221
  53.5 0.8 copy-done.3
  54.6 0.7 copy-done.1
  57.9 53.4 %all-gather = f32[9,16384]{1,0:T(8,128)S(1)} all-gather(f32[9,512]{1,0:T(8,128)S(1)} %concatenate.48), channel_id=2, replica_groups=mesh['gx'=32,'gy'=8] {'gx'}, dimensions={1}, use_global_device_ids=true | all-gather | bytes 608256 | tf_op jit(solution)/shard_map/all_gather | solution.py:193
  111.3 1.0 slice_reduce_fusion.4
  113.1 0.8 maximum_divide_fusion
  (147 shorter events, 18.7 us)
Async XLA Ops:
  0.6 3.0 %copy-start.10 = (f32[128,512]{1,0:T(8,128)S(1)}, f32[128,512]{1,0:T(8,128)}, u32[]{:S(2)}) copy-start(f32[128,512]{1,0:T(8,128)} %param.8) | copy-start | bytes 786436
  0.6 3.0 %copy-start.6 = (s32[128,512]{1,0:T(8,128)S(1)}, s32[128,512]{1,0:T(8,128)}, u32[]{:S(2)}) copy-start(s32[128,512]{1,0:T(8,128)} %param.9) | copy-start | bytes 786436
  3.7 5.3 %collective-permute-start = (f32[5,2,512]{2,1,0:T(2,128)S(1)}, f32[5,2,512]{2,1,0:T(2,128)S(1)}, u32[]{:S(2)}, u32[]{:S(2)}) collective-permute-start(f32[5,2,512]{2,1,0:T(2,128)S(1)} %get-tuple-element.274), channel_id=1, source_target_pairs={{0,8},{8,16},{16,24},{24,32},{32,40},{40,48},{48,56},{56,64},{64,7... | collective-permute-start | bytes 61448 | tf_op jit(solution)/shard_map/ppermute | solution.py:16
  7.6 5.7 %collective-permute-start.1 = (f32[5,2,512]{2,1,0:T(2,128)S(1)}, f32[5,2,512]{2,1,0:T(2,128)S(1)}, u32[]{:S(2)}, u32[]{:S(2)}) collective-permute-start(f32[5,2,512]{2,1,0:T(2,128)S(1)} %get-tuple-element.275), channel_id=1, source_target_pairs={{8,0},{16,8},{24,16},{32,24},{40,32},{48,40},{56,48},{64,56},{72,6... | collective-permute-start | bytes 61448 | tf_op jit(solution)/shard_map/ppermute | solution.py:19
  13.6 8.6 %collective-permute-start.2 = (f32[5,132,2]{2,1,0:T(8,128)S(1)}, f32[5,132,2]{2,1,0:T(8,128)S(1)}, u32[]{:S(2)}, u32[]{:S(2)}) collective-permute-start(f32[5,132,2]{2,1,0:T(8,128)S(1)} %get-tuple-element.272), channel_id=1, source_target_pairs={{0,1},{1,2},{2,3},{3,4},{4,5},{5,6},{6,7},{8,9},{9,10},{10,11},{11... | collective-permute-start | bytes 15848 | tf_op jit(solution)/shard_map/ppermute | solution.py:16
  15.5 8.4 %collective-permute-start.3 = (f32[5,132,2]{2,1,0:T(8,128)S(1)}, f32[5,132,2]{2,1,0:T(8,128)S(1)}, u32[]{:S(2)}, u32[]{:S(2)}) collective-permute-start(f32[5,132,2]{2,1,0:T(8,128)S(1)} %get-tuple-element.273), channel_id=1, source_target_pairs={{1,0},{2,1},{3,2},{4,3},{5,4},{6,5},{7,6},{9,8},{10,9},{11,10},{12... | collective-permute-start | bytes 15848 | tf_op jit(solution)/shard_map/ppermute | solution.py:19
  26.2 1.0 copy-start
  26.2 1.0 copy-start.7
  40.4 10.1 %all-to-all-start = ((f32[8,9,1,128]{3,2,1,0:T(1,128)}), f32[8,9,1,128]{3,2,1,0:T(1,128)S(1)}, u32[]{:S(2)}, u32[]{:S(2)}) async-start(f32[8,9,1,128]{3,2,1,0:T(1,128)} %stack.61), calls=%async_computation | async-start | bytes 73728 | tf_op jit(solution)/shard_map/all_to_all | solution.py:200
  47.4 0.9 copy-start.2
  48.3 0.7 copy-start.4
  51.0 2.5 %copy-start.8 = (f32[1,127,512]{2,1,0:T(8,128)S(1)}, f32[1,127,512]{2,1,0:T(8,128)}, u32[]{:S(2)}) copy-start(f32[1,127,512]{2,1,0:T(8,128)} %get-tuple-element.291) | copy-start | bytes 780292
  51.0 2.5 %copy-start.9 = (f32[1,127,512]{2,1,0:T(8,128)S(1)}, f32[1,127,512]{2,1,0:T(8,128)}, u32[]{:S(2)}) copy-start(f32[1,127,512]{2,1,0:T(8,128)} %get-tuple-element.292) | copy-start | bytes 780292
  53.4 0.9 copy-start.3
  53.4 1.0 copy-start.5
  54.4 0.9 copy-start.1
